TPU v7x, 32 devices: a whole 2x2x4 slice. The times are simulated.
32 devices in a mesh: gx: 4 (over z), gy: 8 (over y, x, core).
Axes of the slice: x: 2, y: 2, z: 4, core: 2. Of those that a mesh axis runs over, the one named last changes fastest.
Arguments:
- patches: bfloat16 [39168, 768], P(('gx', 'gy')), may hold values from -6 to 6
- lengths: int32 [32], P(('gx', 'gy')), may hold values from 122 to 1224, as said below
- cotangent: bfloat16 [39168, 768], P(('gx', 'gy')), may hold values from -6 to 6
- w_qkv: bfloat16 [768, 2304], P('gx', 'gy'), may hold values from -0.21875 to 0.21875
- w_out: bfloat16 [768, 768], P('gx', 'gy'), may hold values from -4 to 4
- w_up: bfloat16 [768, 3072], P('gx', 'gy'), may hold values from -0.21875 to 0.21875
- w_down: bfloat16 [3072, 768], P('gx', 'gy'), may hold values from -0.109375 to 0.109375
- bias_q: bfloat16 [768], P(('gx', 'gy')), may hold values from -3 to 3
- bias_v: bfloat16 [768], P(('gx', 'gy')), may hold values from -3 to 3
- bias_o: bfloat16 [768], P(('gx', 'gy')), may hold values from -1.75 to 1.75
- bias_up: bfloat16 [3072], P(('gx', 'gy')), may hold values from -3 to 3
- bias_down: bfloat16 [768], P(('gx', 'gy')), may hold values from -1.75 to 1.75
- gain_one: bfloat16 [768], P(('gx', 'gy')), may hold values from 0.5 to 1.5
- shift_one: bfloat16 [768], P(('gx', 'gy')), may hold values from -1.75 to 1.75
- gain_two: bfloat16 [768], P(('gx', 'gy')), may hold values from 0.5 to 1.5
- shift_two: bfloat16 [768], P(('gx', 'gy')), may hold values from -1.75 to 1.75
Outputs:
- out_rows: bfloat16 [39168, 768], P(('gx', 'gy'))
- grad_rows: float32 [39168, 768], P(('gx', 'gy'))
- grad_w_qkv: float32 [768, 2304], P('gx', 'gy')
- grad_w_out: float32 [768, 768], P('gx', 'gy')
- grad_w_up: float32 [768, 3072], P('gx', 'gy')
- grad_w_down: float32 [3072, 768], P('gx', 'gy')
- grad_bias_q: float32 [768], P(('gx', 'gy'))
- grad_bias_v: float32 [768], P(('gx', 'gy'))
- grad_bias_o: float32 [768], P(('gx', 'gy'))
- grad_bias_up: float32 [3072], P(('gx', 'gy'))
- grad_bias_down: float32 [768], P(('gx', 'gy'))
- grad_gain_one: float32 [768], P(('gx', 'gy'))
- grad_shift_one: float32 [768], P(('gx', 'gy'))
- grad_gain_two: float32 [768], P(('gx', 'gy'))
- grad_shift_two: float32 [768], P(('gx', 'gy'))
Inputs may be any that keep to these rules, and one draw needn't show every extreme that they name: `lengths`: each clip's true patch count; some clip fills all 1224 slots and some clip has 122 patches in every draw.
All inputs are finite; a program needn't handle non-finite values.
Results may differ from a plain program's by a relative error of at most 0.02.
Values may be sent and summed in bfloat16 or wider, within the bound.
No kernel may reach another device: no remote copies, remote signals or barrier semaphores. Data moves between devices by JAX's collectives and lax.ppermute only.
A program may use at most 192 MiB of HBM per device.

v0:
```python
import jax
import jax.numpy as jnp
from jax import lax
from jax.sharding import PartitionSpec as P

HEADS = 12
HEAD_DIM = 64
EPSILON = 1e-06
NEG_FILL = -1e30


def layer_norm(values, gain_vec, shift_vec):
    centre = values - jnp.mean(values, axis=-1, keepdims=True)
    spread = jnp.mean(centre * centre, axis=-1, keepdims=True)
    return centre * lax.rsqrt(spread + EPSILON) * gain_vec + shift_vec


def exact_gelu(values):
    return jax.nn.gelu(values, approximate=False)


def to_blocks(columns, clip_count, pair_count):
    slot_count = columns.shape[0] // clip_count
    pair_width = columns.shape[1] // pair_count
    shaped = columns.reshape(clip_count, slot_count, pair_count, pair_width)
    return jnp.transpose(shaped, (0, 2, 1, 3)).reshape(
        clip_count * pair_count, slot_count, pair_width
    )


def from_blocks(blocks_in, clip_count, pair_count):
    slot_count = blocks_in.shape[1]
    pair_width = blocks_in.shape[2]
    shaped = blocks_in.reshape(clip_count, pair_count, slot_count, pair_width)
    return jnp.transpose(shaped, (0, 2, 1, 3)).reshape(
        clip_count * slot_count, pair_count * pair_width
    )


def block_scores(queries, key_rows, length):
    slot_count = queries.shape[0]
    query_heads = queries.reshape(slot_count, 2, HEAD_DIM)
    key_heads = key_rows.reshape(slot_count, 2, HEAD_DIM)
    scores = jnp.einsum(
        "qhd,khd->hqk", query_heads, key_heads, preferred_element_type=jnp.float32
    ) * HEAD_DIM ** (-0.5)
    live_keys = jnp.arange(slot_count) < length
    return (jnp.where(live_keys[None, None, :], scores, NEG_FILL), query_heads, key_heads)


def attend(block_in):
    queries, key_rows, values, length = block_in
    scores, query_heads, key_heads = block_scores(queries, key_rows, length)
    maximum = jnp.max(scores, axis=-1, keepdims=True)
    exponent = jnp.exp(scores - maximum)
    summed = jnp.sum(exponent, axis=-1, keepdims=True)
    weights = (exponent / summed).astype(jnp.bfloat16)
    value_heads = values.reshape(values.shape[0], 2, HEAD_DIM)
    mixed_heads = jnp.einsum(
        "hqk,khd->qhd", weights, value_heads, preferred_element_type=jnp.float32
    )
    return (
        mixed_heads.reshape(queries.shape[0], 2 * HEAD_DIM),
        (maximum + jnp.log(summed))[..., 0],
    )


def attend_back(block_in):
    queries, key_rows, values, grad_out, log_total, length = block_in
    slot_count = queries.shape[0]
    scores, query_heads, key_heads = block_scores(queries, key_rows, length)
    weights = jnp.exp(scores - log_total[..., None])
    value_heads = values.reshape(slot_count, 2, HEAD_DIM)
    grad_heads = grad_out.reshape(slot_count, 2, HEAD_DIM)
    d_weights = jnp.einsum(
        "qhd,khd->hqk", grad_heads, value_heads, preferred_element_type=jnp.float32
    )
    d_values = jnp.einsum(
        "hqk,qhd->khd", weights.astype(jnp.bfloat16), grad_heads, preferred_element_type=jnp.float32
    )
    row_dots = jnp.sum(weights * d_weights, axis=-1, keepdims=True)
    d_scores = (weights * (d_weights - row_dots)).astype(jnp.bfloat16)
    d_queries = jnp.einsum(
        "hqk,khd->qhd", d_scores, key_heads, preferred_element_type=jnp.float32
    ) * HEAD_DIM ** (-0.5)
    d_keys = jnp.einsum(
        "hqk,qhd->khd", d_scores, query_heads, preferred_element_type=jnp.float32
    ) * HEAD_DIM ** (-0.5)
    return (
        d_queries.reshape(slot_count, 2 * HEAD_DIM),
        d_keys.reshape(slot_count, 2 * HEAD_DIM),
        d_values.reshape(slot_count, 2 * HEAD_DIM),
    )


def per_device(
    patches,
    lengths,
    cotangent,
    w_qkv,
    w_out,
    w_up,
    w_down,
    bias_q,
    bias_v,
    bias_o,
    bias_up,
    bias_down,
    gain_one,
    shift_one,
    gain_two,
    shift_two,
):
    by_cols = (
        lax.all_gather(w_qkv, "gy", axis=1, tiled=True),
        lax.all_gather(w_out, "gy", axis=1, tiled=True),
        lax.all_gather(w_up, "gy", axis=1, tiled=True),
        lax.all_gather(w_down, "gy", axis=1, tiled=True),
        lax.all_gather(bias_q, "gy", axis=0, tiled=True),
        lax.all_gather(bias_v, "gy", axis=0, tiled=True),
        lax.all_gather(bias_o, "gy", axis=0, tiled=True),
        lax.all_gather(bias_up, "gy", axis=0, tiled=True),
        lax.all_gather(bias_down, "gy", axis=0, tiled=True),
        lax.all_gather(gain_one, "gy", axis=0, tiled=True),
        lax.all_gather(shift_one, "gy", axis=0, tiled=True),
        lax.all_gather(gain_two, "gy", axis=0, tiled=True),
        lax.all_gather(shift_two, "gy", axis=0, tiled=True),
    )
    gathered = (
        lax.all_gather(by_cols[0], "gx", axis=0, tiled=True),
        lax.all_gather(by_cols[1], "gx", axis=0, tiled=True),
        lax.all_gather(by_cols[2], "gx", axis=0, tiled=True),
        lax.all_gather(by_cols[3], "gx", axis=0, tiled=True),
        lax.all_gather(by_cols[4], "gx", axis=0, tiled=True),
        lax.all_gather(by_cols[5], "gx", axis=0, tiled=True),
        lax.all_gather(by_cols[6], "gx", axis=0, tiled=True),
        lax.all_gather(by_cols[7], "gx", axis=0, tiled=True),
        lax.all_gather(by_cols[8], "gx", axis=0, tiled=True),
        lax.all_gather(by_cols[9], "gx", axis=0, tiled=True),
        lax.all_gather(by_cols[10], "gx", axis=0, tiled=True),
        lax.all_gather(by_cols[11], "gx", axis=0, tiled=True),
        lax.all_gather(by_cols[12], "gx", axis=0, tiled=True),
    )
    mat_qkv, mat_out, mat_up, mat_down = (gathered[0], gathered[1], gathered[2], gathered[3])
    vec_q, vec_v, vec_o, vec_up, vec_down, gain_a, shift_a, gain_b, shift_b = [
        member.astype(jnp.float32) for member in gathered[4:]
    ]
    clip_count = lengths.shape[0]
    slot_count = patches.shape[0] // clip_count
    model_width = patches.shape[1]
    pair_count = HEADS // 2
    inputs32 = patches.astype(jnp.float32)
    normed, norm_pull = jax.vjp(layer_norm, inputs32, gain_a, shift_a)
    normed_low = normed.astype(jnp.bfloat16)
    bias_all = jnp.concatenate([vec_q, jnp.zeros_like(vec_q), vec_v])
    project = (jnp.dot(normed_low, mat_qkv, preferred_element_type=jnp.float32) + bias_all).astype(
        jnp.bfloat16
    )
    query_blocks = to_blocks(project[:, :model_width], clip_count, pair_count)
    key_blocks = to_blocks(project[:, model_width : 2 * model_width], clip_count, pair_count)
    value_blocks = to_blocks(project[:, 2 * model_width :], clip_count, pair_count)
    pair_lengths = jnp.repeat(lengths, pair_count)
    mixed_blocks, total_blocks = lax.map(
        attend, (query_blocks, key_blocks, value_blocks, pair_lengths)
    )
    mixed_low = from_blocks(mixed_blocks, clip_count, pair_count).astype(jnp.bfloat16)
    residual = inputs32 + jnp.dot(mixed_low, mat_out, preferred_element_type=jnp.float32) + vec_o
    normed_two, norm_pull_two = jax.vjp(layer_norm, residual, gain_b, shift_b)
    normed_two_low = normed_two.astype(jnp.bfloat16)
    inner_pre = jnp.dot(normed_two_low, mat_up, preferred_element_type=jnp.float32) + vec_up
    active, gelu_pull = jax.vjp(exact_gelu, inner_pre)
    active_low = active.astype(jnp.bfloat16)
    outputs = (
        residual + jnp.dot(active_low, mat_down, preferred_element_type=jnp.float32) + vec_down
    ).astype(jnp.bfloat16)
    regather_cols = (
        lax.all_gather(w_qkv, "gy", axis=1, tiled=True),
        lax.all_gather(w_out, "gy", axis=1, tiled=True),
        lax.all_gather(w_up, "gy", axis=1, tiled=True),
        lax.all_gather(w_down, "gy", axis=1, tiled=True),
    )
    regathered = (
        lax.all_gather(regather_cols[0], "gx", axis=0, tiled=True),
        lax.all_gather(regather_cols[1], "gx", axis=0, tiled=True),
        lax.all_gather(regather_cols[2], "gx", axis=0, tiled=True),
        lax.all_gather(regather_cols[3], "gx", axis=0, tiled=True),
    )
    back_qkv, back_out, back_up, back_down = (
        regathered[0],
        regathered[1],
        regathered[2],
        regathered[3],
    )
    live_rows = (
        (jnp.arange(slot_count)[None, :] < lengths[:, None]).astype(jnp.float32).reshape(-1, 1)
    )
    seed_grad = cotangent.astype(jnp.float32) * live_rows
    seed_low = seed_grad.astype(jnp.bfloat16)
    grad_bias_down = jnp.sum(seed_grad, axis=0)
    grad_w_down = jnp.einsum("tf,td->fd", active_low, seed_low, preferred_element_type=jnp.float32)
    d_active = jnp.einsum("td,fd->tf", seed_low, back_down, preferred_element_type=jnp.float32)
    d_inner = gelu_pull(d_active)[0].astype(jnp.bfloat16)
    grad_bias_up = jnp.sum(d_inner.astype(jnp.float32), axis=0)
    grad_w_up = jnp.einsum("td,tf->df", normed_two_low, d_inner, preferred_element_type=jnp.float32)
    d_normed_two = jnp.einsum("tf,df->td", d_inner, back_up, preferred_element_type=jnp.float32)
    d_resid_norm, grad_gain_two, grad_shift_two = norm_pull_two(d_normed_two)
    d_residual = seed_grad + d_resid_norm
    grad_bias_o = jnp.sum(d_residual, axis=0)
    d_branch = d_residual.astype(jnp.bfloat16)
    grad_w_out = jnp.einsum("te,td->ed", mixed_low, d_branch, preferred_element_type=jnp.float32)
    d_mixed = jnp.einsum(
        "td,ed->te", d_branch, back_out, preferred_element_type=jnp.float32
    ).astype(jnp.bfloat16)
    grad_blocks = to_blocks(d_mixed, clip_count, pair_count)
    d_queries, d_keys, d_values = lax.map(
        attend_back,
        (query_blocks, key_blocks, value_blocks, grad_blocks, total_blocks, pair_lengths),
    )
    d_project = jnp.concatenate(
        [
            from_blocks(d_queries, clip_count, pair_count),
            from_blocks(d_keys, clip_count, pair_count),
            from_blocks(d_values, clip_count, pair_count),
        ],
        axis=1,
    ).astype(jnp.bfloat16)
    column_sums = jnp.sum(d_project.astype(jnp.float32), axis=0)
    grad_bias_q = column_sums[:model_width]
    grad_bias_v = column_sums[2 * model_width :]
    grad_w_qkv = jnp.einsum("td,te->de", normed_low, d_project, preferred_element_type=jnp.float32)
    d_normed = jnp.einsum("te,de->td", d_project, back_qkv, preferred_element_type=jnp.float32)
    d_input_norm, grad_gain_one, grad_shift_one = norm_pull(d_normed)
    grad_rows = d_residual + d_input_norm
    section_one = (
        lax.psum_scatter(
            grad_w_qkv.astype(jnp.bfloat16), "gx", scatter_dimension=0, tiled=True
        ).astype(jnp.float32),
        lax.psum_scatter(
            grad_w_out.astype(jnp.bfloat16), "gx", scatter_dimension=0, tiled=True
        ).astype(jnp.float32),
        lax.psum_scatter(
            grad_w_up.astype(jnp.bfloat16), "gx", scatter_dimension=0, tiled=True
        ).astype(jnp.float32),
        lax.psum_scatter(
            grad_w_down.astype(jnp.bfloat16), "gx", scatter_dimension=0, tiled=True
        ).astype(jnp.float32),
        lax.psum_scatter(
            grad_bias_q.astype(jnp.bfloat16), "gx", scatter_dimension=0, tiled=True
        ).astype(jnp.float32),
        lax.psum_scatter(
            grad_bias_v.astype(jnp.bfloat16), "gx", scatter_dimension=0, tiled=True
        ).astype(jnp.float32),
        lax.psum_scatter(
            grad_bias_o.astype(jnp.bfloat16), "gx", scatter_dimension=0, tiled=True
        ).astype(jnp.float32),
        lax.psum_scatter(
            grad_bias_up.astype(jnp.bfloat16), "gx", scatter_dimension=0, tiled=True
        ).astype(jnp.float32),
        lax.psum_scatter(
            grad_bias_down.astype(jnp.bfloat16), "gx", scatter_dimension=0, tiled=True
        ).astype(jnp.float32),
        lax.psum_scatter(
            grad_gain_one.astype(jnp.bfloat16), "gx", scatter_dimension=0, tiled=True
        ).astype(jnp.float32),
        lax.psum_scatter(
            grad_shift_one.astype(jnp.bfloat16), "gx", scatter_dimension=0, tiled=True
        ).astype(jnp.float32),
        lax.psum_scatter(
            grad_gain_two.astype(jnp.bfloat16), "gx", scatter_dimension=0, tiled=True
        ).astype(jnp.float32),
        lax.psum_scatter(
            grad_shift_two.astype(jnp.bfloat16), "gx", scatter_dimension=0, tiled=True
        ).astype(jnp.float32),
    )
    reduced = (
        lax.psum_scatter(
            section_one[0].astype(jnp.bfloat16), "gy", scatter_dimension=1, tiled=True
        ).astype(jnp.float32),
        lax.psum_scatter(
            section_one[1].astype(jnp.bfloat16), "gy", scatter_dimension=1, tiled=True
        ).astype(jnp.float32),
        lax.psum_scatter(
            section_one[2].astype(jnp.bfloat16), "gy", scatter_dimension=1, tiled=True
        ).astype(jnp.float32),
        lax.psum_scatter(
            section_one[3].astype(jnp.bfloat16), "gy", scatter_dimension=1, tiled=True
        ).astype(jnp.float32),
        lax.psum_scatter(
            section_one[4].astype(jnp.bfloat16), "gy", scatter_dimension=0, tiled=True
        ).astype(jnp.float32),
        lax.psum_scatter(
            section_one[5].astype(jnp.bfloat16), "gy", scatter_dimension=0, tiled=True
        ).astype(jnp.float32),
        lax.psum_scatter(
            section_one[6].astype(jnp.bfloat16), "gy", scatter_dimension=0, tiled=True
        ).astype(jnp.float32),
        lax.psum_scatter(
            section_one[7].astype(jnp.bfloat16), "gy", scatter_dimension=0, tiled=True
        ).astype(jnp.float32),
        lax.psum_scatter(
            section_one[8].astype(jnp.bfloat16), "gy", scatter_dimension=0, tiled=True
        ).astype(jnp.float32),
        lax.psum_scatter(
            section_one[9].astype(jnp.bfloat16), "gy", scatter_dimension=0, tiled=True
        ).astype(jnp.float32),
        lax.psum_scatter(
            section_one[10].astype(jnp.bfloat16), "gy", scatter_dimension=0, tiled=True
        ).astype(jnp.float32),
        lax.psum_scatter(
            section_one[11].astype(jnp.bfloat16), "gy", scatter_dimension=0, tiled=True
        ).astype(jnp.float32),
        lax.psum_scatter(
            section_one[12].astype(jnp.bfloat16), "gy", scatter_dimension=0, tiled=True
        ).astype(jnp.float32),
    )
    return (
        outputs,
        grad_rows,
        reduced[0],
        reduced[1],
        reduced[2],
        reduced[3],
        reduced[4],
        reduced[5],
        reduced[6],
        reduced[7],
        reduced[8],
        reduced[9],
        reduced[10],
        reduced[11],
        reduced[12],
    )


def solution(mesh):
    in_specs = (
        P(("gx", "gy"), None),
        P(("gx", "gy")),
        P(("gx", "gy"), None),
        P("gx", "gy"),
        P("gx", "gy"),
        P("gx", "gy"),
        P("gx", "gy"),
        P(("gx", "gy")),
        P(("gx", "gy")),
        P(("gx", "gy")),
        P(("gx", "gy")),
        P(("gx", "gy")),
        P(("gx", "gy")),
        P(("gx", "gy")),
        P(("gx", "gy")),
        P(("gx", "gy")),
    )
    out_specs = (
        P(("gx", "gy"), None),
        P(("gx", "gy"), None),
        P("gx", "gy"),
        P("gx", "gy"),
        P("gx", "gy"),
        P("gx", "gy"),
        P(("gx", "gy")),
        P(("gx", "gy")),
        P(("gx", "gy")),
        P(("gx", "gy")),
        P(("gx", "gy")),
        P(("gx", "gy")),
        P(("gx", "gy")),
        P(("gx", "gy")),
        P(("gx", "gy")),
    )
    return jax.shard_map(
        per_device, mesh=mesh, in_specs=in_specs, out_specs=out_specs, check_vma=False
    )
```

profile of v0, /device:TPU:0, one launch (start us, length us, event | category | flops | bytes accessed | tf_op | source)
XLA Modules:
  0.0 970.7 jit_solution(14444285091718010703)
XLA Ops:
  10.0 13.0 %all_gather.90 = bf16[192,2304]{0,1:T(8,128)(2,1)S(1)} all-gather(bf16[192,288]{0,1:T(8,128)(2,1)S(1)} %copy.64), channel_id=1, replica_groups=mesh['gx'=4,'gy'=8] {'gy'}, dimensions={1}, use_global_device_ids=true | all-gather | bytes 995328 | tf_op jit(solution)/shard_map/all_gather | solution.py:115
  24.5 10.5 %all_gather.96 = bf16[192,768]{0,1:T(8,128)(2,1)S(1)} all-gather(bf16[192,96]{0,1:T(8,128)(2,1)S(1)} %copy.69), channel_id=1, replica_groups=mesh['gx'=4,'gy'=8] {'gy'}, dimensions={1}, use_global_device_ids=true | all-gather | bytes 331776 | tf_op jit(solution)/shard_map/all_gather | solution.py:116
  42.0 13.4 %all-reduce.36 = (bf16[768]{0:T(1024)(128)(2,1)S(1)}, bf16[192]{0:T(256)(128)(2,1)S(1)}, bf16[192]{0:T(256)(128)(2,1)S(1)}, bf16[192]{0:T(256)(128)(2,1)S(1)}, b...) all-reduce(bf16[768]{0:T(1024)(128)(2,1)S(1)} %dynamic-update-slice, ...), channel_id=1, replica_groups=mesh['gx'=4,'gy'=8] {'gy'}, use_global_device_ids=true, to_apply=%add.14 | all-reduce | flops 2112 | bytes 8448
  56.9 19.1 %all-reduce.38 = (bf16[768]{0:T(1024)(128)(2,1)S(1)}, bf16[768]{0:T(1024)(128)(2,1)S(1)}, bf16[768]{0:T(1024)(128)(2,1)S(1)}, bf16[768]{0:T(1024)(128)(2,1)S(1)}...) all-reduce(bf16[768]{0:T(1024)(128)(2,1)S(1)} %dynamic-update-slice, ...), channel_id=1, replica_groups=mesh['gx'=4,'gy'=8] {'gx'}, use_global_device_ids=true, to_apply=%add.7 | all-reduce | flops 5376 | bytes 21504
  76.8 13.6 %all-gather = bf16[4,1,768]{2,1,0:T(2,128)(2,1)S(1)} all-gather(bf16[1,1,768]{2,1,0:T(2,128)(2,1)S(1)} %reshape.302), channel_id=1, replica_groups=mesh['gx'=4,'gy'=8] {'gx'}, dimensions={0}, use_global_device_ids=true | all-gather | bytes 7680 | tf_op jit(solution)/shard_map/all_gather | solution.py:137
  93.0 43.1 %all-gather.8.cloned.1.call-done = bf16[768,2304]{1,0:T(8,128)(2,1)} async-done(((bf16[192,2304]{1,0:T(8,128)(2,1)}), bf16[768,2304]{1,0:T(8,128)(2,1)}) %all-gather.8.cloned.1.call-update) | async-done | bytes 3538960 | tf_op jit(solution)/shard_map/all_gather | solution.py:130
  136.1 7.4 fusion.14
  159.5 65.9 %while.26 = (s32[]{:T(128)}, bf16[6,1224,128]{1,2,0:T(8,128)(2,1)}, f32[6,2,1224]{2,1,0:T(2,128)}, bf16[6,1224,128]{1,2,0:T(8,128)(2,1)}, s32[6]{0:T(128)S(1)}, ...) while((s32[]{:T(128)}, bf16[6,1224,128]{1,2,0:T(8,128)(2,1)}, ...), condition=%wide.region_5.6_spmd, body=%wide.region_2.5_spmd.sunk | while | flops 791035712 | bytes 39813052 | solution.py:163
  231.7 25.5 %all-gather.14.cloned.1.call-done = bf16[768,3072]{1,0:T(8,128)(2,1)} async-done(((bf16[192,3072]{1,0:T(8,128)(2,1)}), bf16[768,3072]{1,0:T(8,128)(2,1)}) %all-gather.14.cloned.1.call-update) | async-done | bytes 4718608 | tf_op jit(solution)/shard_map/all_gather | solution.py:132
  257.2 42.4 %multiply_convert_fusion.1 = (bf16[1224,3072]{1,0:T(8,128)(2,1)}, f32[1224,3072]{1,0:T(8,128)}, f32[1224,3072]{1,0:T(8,128)}) fusion(f32[3072]{0:T(1024)S(1)} %bitcast.196, bf16[768,3072]{1,0:T(8,128)(2,1)} %all-gather.14.cloned.1.call-done, f32[1224,768]{1,0:T(8,128)} %copy-done.2, f32[768]{0:T(1024)S(1)} %convert_element_type.206, ...), kind=kOutput, calls=%fused_computation.34 | convolution fusion | flops 6028425216 | bytes 46108224 | tf_op jit(solution)/shard_map/dot_general | solution.py:170
  299.6 46.9 %all-gather.18.cloned.1.call-done = bf16[3072,768]{0,1:T(8,128)(2,1)} async-done(((bf16[768,768]{0,1:T(8,128)(2,1)}), bf16[3072,768]{0,1:T(8,128)(2,1)}) %all-gather.18.cloned.1.call-update) | async-done | bytes 4718608 | tf_op jit(solution)/shard_map/all_gather | solution.py:133
  346.5 19.9 %fusion.53 = (bf16[3072]{0:T(1024)(128)(2,1)}, bf16[1224,3072]{1,0:T(8,128)(2,1)}) fusion(f32[1224,3072]{1,0:T(8,128)} %get-tuple-element.252, f32[1224,3072]{1,0:T(8,128)} %get-tuple-element.273, bf16[3072,768]{0,1:T(8,128)(2,1)} %all-gather.18.cloned.1.call-done, bf16[1224,768]{1,0:T(8,128)(2,1)S(1)} %copy-done.7, f32[1224]{0:T(1024)S(1)} %copy-done.21), kind=kOutput, calls=%fused_computation.122 | convolution fusion | flops 5834775552 | bytes 44210976 | tf_op jit(solution)/shard_map/td,fd->tf/dot_general | solution.py:201
  366.4 12.7 %multiply_reduce_fusion.1 = (bf16[768]{0:T(1024)(128)(2,1)}, f32[1224]{0:T(1024)S(1)}, bf16[768]{0:T(1024)(128)(2,1)}, f32[1224,768]{1,0:T(8,128)S(1)}) fusion(f32[1224,768]{1,0:T(8,128)} %copy-done.2, f32[1224]{0:T(1024)S(1)} %fusion.37, f32[1224]{0:T(1024)S(1)} %broadcast_multiply_fusion, f32[768]{0:T(1024)S(1)} %convert_element_type.205, ...), kind=kOutput, calls=%fused_computation.74 | convolution fusion | flops 5783073792 | bytes 19779936 | tf_op jit(solution)/shard_map/tf,df->td/dot_general | solution.py:205
  399.1 150.7 %while.27 = (s32[]{:T(128)}, bf16[6,1224,128]{1,2,0:T(8,128)(2,1)}, bf16[6,1224,128]{1,2,0:T(8,128)(2,1)}, bf16[6,1224,128]{1,2,0:T(8,128)(2,1)}, bf16[6,1224,12...) while((s32[]{:T(128)}, bf16[6,1224,128]{1,2,0:T(8,128)(2,1)}, ...), condition=%wide.region_12.13_spmd, body=%wide.region_10.12_spmd.sunk | while | flops 1945257856 | bytes 116307088 | solution.py:215
  414.6 4.9 convolution_multiply_fusion.7
  464.7 4.9 convolution_multiply_fusion.7
  549.9 10.0 %convolution_convert_fusion = bf16[768,2304]{1,0:T(8,128)(2,1)} fusion(bf16[1224,768]{1,0:T(8,128)(2,1)S(1)} %copy-done.1, f32[768]{0:T(1024)S(1)} %copy-done.33, f32[768]{0:T(1024)S(1)} %copy-done.20, f32[1224]{0:T(1024)S(1)} %copy-done.15, f32[1224]{0:T(1024)S(1)} %copy-done.9, bf16[1224,768]{0,1:T(8,128)(2,1)} %bitcast.184, ...), kind=kOutput, calls=%fused_computation.61 | convolution fusion | flops 4355997696 | bytes 11075136 | tf_op jit(solution)/shard_map/td,te->de/dot_general | solution.py:230
  560.0 12.1 %convolution_convert_fusion.2 = bf16[768,3072]{1,0:T(8,128)(2,1)} fusion(bf16[1224,3072]{1,0:T(8,128)(2,1)} %get-tuple-element.277, f32[1224,768]{1,0:T(8,128)} %copy-done.2, f32[768]{0:T(1024)S(1)} %copy-done.31, f32[768]{0:T(1024)S(1)} %copy-done.28, f32[1224]{0:T(1024)S(1)} %copy-done.26, f32[1224]{0:T(1024)S(1)} %copy-done.17), kind=kOutput, calls=%fused_computation.63 | convolution fusion | flops 5782616064 | bytes 16014912 | tf_op jit(solution)/shard_map/td,tf->df/dot_general | solution.py:204
  572.9 11.4 %convolution_convert_fusion.1 = bf16[3072,768]{1,0:T(8,128)(2,1)} fusion(bf16[1224,3072]{1,0:T(8,128)(2,1)} %get-tuple-element.251, bf16[1224,768]{1,0:T(8,128)(2,1)} %param.22, f32[1224]{0:T(1024)S(1)} %copy-done.22), kind=kOutput, calls=%fused_computation.62 | convolution fusion | flops 5780736000 | bytes 14123808 | tf_op jit(solution)/shard_map/tf,td->fd/dot_general | solution.py:200
  589.1 10.0 %fusion.44 = (bf16[768]{0:T(1024)(128)(2,1)S(1)}, f32[1224]{0:T(1024)S(1)}, f32[1224,768]{1,0:T(8,128)}) fusion(f32[768]{0:T(1024)S(1)} %copy-done.20, f32[1224]{0:T(1024)S(1)} %copy-done.9, bf16[1224,768]{1,0:T(8,128)(2,1)S(1)} %copy-done.1, bf16[768,2304]{1,0:T(8,128)(2,1)} %all-gather.8.cloned.1.call-done, bf16[1224,768]{0,1:T(8,128)(2,1)} %bitcast.185, ...), kind=kOutput, calls=%fused_computation.114 | convolution fusion | flops 4354226176 | bytes 14833728 | tf_op jit(solution)/shard_map/te,de->td/dot_general | solution.py:231
  599.1 25.7 %reduce-scatter.17.cloned.1.call-done = bf16[192,2304]{1,0:T(8,128)(2,1)} async-done(((bf16[768,2304]{1,0:T(8,128)(2,1)}), bf16[192,2304]{1,0:T(8,128)(2,1)}) %reduce-scatter.17.cloned.1.call-update) | async-done | bytes 884752 | tf_op jit(solution)/shard_map/reduce_scatter | solution.py:235
  633.5 79.2 %reduce-scatter.21.cloned.1.call-done = bf16[192,3072]{1,0:T(8,128)(2,1)} async-done(((bf16[768,3072]{1,0:T(8,128)(2,1)}), bf16[192,3072]{1,0:T(8,128)(2,1)}) %reduce-scatter.21.cloned.1.call-update) | async-done | bytes 1179664 | tf_op jit(solution)/shard_map/reduce_scatter | solution.py:241
  715.4 7.2 fusion.28
  722.7 19.6 %all-reduce.37 = (bf16[768]{0:T(1024)(128)(2,1)S(1)}, bf16[768]{0:T(1024)(128)(2,1)S(1)}, bf16[768]{0:T(1024)(128)(2,1)S(1)}, bf16[3072]{0:T(1024)(128)(2,1)S(1)...) all-reduce(bf16[768]{0:T(1024)(128)(2,1)S(1)} %get-tuple-element.26, ...), channel_id=10, replica_groups=mesh['gx'=4,'gy'=8] {'gx'}, use_global_device_ids=true, to_apply=%region_24.25.clone | all-reduce | flops 9216 | bytes 36864
  742.9 13.2 %all-reduce.35 = (bf16[192]{0:T(256)(128)(2,1)S(1)}, bf16[192]{0:T(256)(128)(2,1)S(1)}, bf16[192]{0:T(256)(128)(2,1)S(1)}, bf16[192]{0:T(256)(128)(2,1)S(1)}, bf...) all-reduce(bf16[192]{0:T(256)(128)(2,1)S(1)} %dynamic-update-slice., ...), channel_id=1, replica_groups=mesh['gx'=4,'gy'=8] {'gy'}, use_global_device_ids=true, to_apply=%add.15 | all-reduce | flops 2496 | bytes 9984
  756.4 10.7 %all-reduce.16 = bf16[768]{0:T(1024)(128)(2,1)S(1)} all-reduce(bf16[768]{0:T(1024)(128)(2,1)S(1)} %dynamic-update-slice.16), channel_id=1, replica_groups=mesh['gx'=4,'gy'=8] {'gx'}, use_global_device_ids=true, to_apply=%add.16 | all-reduce | flops 768 | bytes 3072
  772.4 29.6 %reduce-scatter.23.cloned.1.call-done = bf16[768,768]{1,0:T(8,128)(2,1)} async-done(((bf16[3072,768]{1,0:T(8,128)(2,1)}), bf16[768,768]{1,0:T(8,128)(2,1)}) %reduce-scatter.23.cloned.1.call-update) | async-done | bytes 1179664 | tf_op jit(solution)/shard_map/reduce_scatter | solution.py:244
  804.4 11.3 %fusion.30 = bf16[1224,768]{1,0:T(8,128)(2,1)} fusion(f32[1224,768]{1,0:T(8,128)} %copy-done.2, bf16[1224,3072]{1,0:T(8,128)(2,1)} %get-tuple-element.251, bf16[3072,768]{0,1:T(8,128)(2,1)} %all-gather.18.cloned.1.call-done, f32[768]{0:T(1024)S(1)} %convert_element_type.210), kind=kOutput, calls=%fused_computation.83 | convolution fusion | flops 5778376704 | bytes 17882112 | tf_op jit(solution)/shard_map/dot_general | solution.py:174
  815.7 23.8 %reduce-scatter.27.cloned.1.call-done = bf16[96,192]{1,0:T(8,128)(2,1)} async-done(((bf16[768,192]{1,0:T(8,128)(2,1)}), bf16[96,192]{1,0:T(8,128)(2,1)}) %reduce-scatter.27.cloned.1.call-update) | async-done | bytes 36880
  841.1 38.3 %reduce-scatter.25.cloned.1.call-done = bf16[288,192]{1,0:T(8,128)(2,1)} async-done(((bf16[2304,192]{1,0:T(8,128)(2,1)}), bf16[288,192]{1,0:T(8,128)(2,1)}) %reduce-scatter.25.cloned.1.call-update) | async-done | bytes 110608
  881.1 40.4 %reduce-scatter.29.cloned.1.call-done = bf16[384,192]{1,0:T(8,128)(2,1)} async-done(((bf16[3072,192]{1,0:T(8,128)(2,1)}), bf16[384,192]{1,0:T(8,128)(2,1)}) %reduce-scatter.29.cloned.1.call-update) | async-done | bytes 147472
  923.3 38.4 %reduce-scatter.31.cloned.1.call-done = bf16[96,768]{1,0:T(8,128)(2,1)} async-done(((bf16[768,768]{1,0:T(8,128)(2,1)}), bf16[96,768]{1,0:T(8,128)(2,1)}) %reduce-scatter.31.cloned.1.call-update) | async-done | bytes 147472
  (415 shorter events, 291.2 us)
Async XLA Ops:
  7.2 30.1 %all-gather.12.cloned.1.call-start = ((), (), s32[]{:S(2)}) async-start(), calls=%async_computation.10 | async-start | bytes 1327104 | tf_op jit(solution)/shard_map/all_gather | solution.py:117
  8.0 84.7 %all-gather.16.cloned.1.call-start = ((), (), s32[]{:S(2)}) async-start(), calls=%async_computation.12 | async-start | bytes 1327104 | tf_op jit(solution)/shard_map/all_gather | solution.py:118
  8.8 82.3 %copy-start = (bf16[1224,768]{1,0:T(8,128)(2,1)S(1)}, bf16[1224,768]{1,0:T(8,128)(2,1)}, u32[]{:S(2)}) copy-start(bf16[1224,768]{1,0:T(8,128)(2,1)} %param.20) | copy-start | bytes 5640196
  8.8 127.3 %all-gather.8.cloned.1.call-start = ((), (), s32[]{:S(2)}) async-start(), calls=%async_computation.8 | async-start | bytes 4423680 | tf_op jit(solution)/shard_map/all_gather | solution.py:130
  24.4 201.0 %all-gather.10.cloned.1.call-start = ((), (), s32[]{:S(2)}) async-start(), calls=%async_computation.9 | async-start | bytes 1474560 | tf_op jit(solution)/shard_map/all_gather | solution.py:131
  35.9 221.3 %all-gather.14.cloned.1.call-start = ((), (), s32[]{:S(2)}) async-start(), calls=%async_computation.11 | async-start | bytes 5898240 | tf_op jit(solution)/shard_map/all_gather | solution.py:132
  37.4 309.1 %all-gather.18.cloned.1.call-start = ((), (), s32[]{:S(2)}) async-start(), calls=%async_computation.13 | async-start | bytes 5898240 | tf_op jit(solution)/shard_map/all_gather | solution.py:133
  76.1 67.4 %copy-start.19 = (f32[768]{0:T(1024)}, f32[768]{0:T(1024)S(1)}, u32[]{:S(2)}) copy-start(f32[768]{0:T(1024)S(1)} %convert_element_type.194) | copy-start | bytes 9220
  76.1 67.4 %copy-start.32 = (f32[768]{0:T(1024)}, f32[768]{0:T(1024)S(1)}, u32[]{:S(2)}) copy-start(f32[768]{0:T(1024)S(1)} %convert_element_type.195) | copy-start | bytes 9220
  76.8 302.4 %copy-start.27 = (f32[768]{0:T(1024)}, f32[768]{0:T(1024)S(1)}, u32[]{:S(2)}) copy-start(f32[768]{0:T(1024)S(1)} %convert_element_type.205) | copy-start | bytes 9220
  76.8 180.4 %copy-start.30 = (f32[768]{0:T(1024)}, f32[768]{0:T(1024)S(1)}, u32[]{:S(2)}) copy-start(f32[768]{0:T(1024)S(1)} %convert_element_type.206) | copy-start | bytes 9220
  91.4 52.1 %copy-start.8 = (f32[1224]{0:T(1024)}, f32[1224]{0:T(1024)S(1)}, u32[]{:S(2)}) copy-start(f32[1224]{0:T(1024)S(1)} %broadcast_multiply_fusion.1) | copy-start | bytes 14692
  92.7 50.8 %copy-start.14 = (f32[1224]{0:T(1024)}, f32[1224]{0:T(1024)S(1)}, u32[]{:S(2)}) copy-start(f32[1224]{0:T(1024)S(1)} %fusion.36) | copy-start | bytes 14692
  92.7 494.4 %reduce-scatter.19.cloned.1.call-start = ((), (), s32[]{:S(2)}) async-start(), calls=%async_computation.15 | async-start | bytes 1474560 | tf_op jit(solution)/shard_map/reduce_scatter | solution.py:238
  229.2 149.9 %copy-start.16 = (f32[1224]{0:T(1024)}, f32[1224]{0:T(1024)S(1)}, u32[]{:S(2)}) copy-start(f32[1224]{0:T(1024)S(1)} %broadcast_multiply_fusion) | copy-start | bytes 14692
  231.6 147.6 %copy-start.25 = (f32[1224]{0:T(1024)}, f32[1224]{0:T(1024)S(1)}, u32[]{:S(2)}) copy-start(f32[1224]{0:T(1024)S(1)} %fusion.37) | copy-start | bytes 14692
  257.2 89.3 %copy-start.7 = (bf16[1224,768]{1,0:T(8,128)(2,1)S(1)}, bf16[1224,768]{1,0:T(8,128)(2,1)}, u32[]{:S(2)}) copy-start(bf16[1224,768]{1,0:T(8,128)(2,1)} %param.22) | copy-start | bytes 5640196
  257.2 89.3 %copy-start.21 = (f32[1224]{0:T(1024)S(1)}, f32[1224]{0:T(1024)}, u32[]{:S(2)}) copy-start(f32[1224]{0:T(1024)} %fusion.35) | copy-start | bytes 14692
  387.6 237.2 %reduce-scatter.17.cloned.1.call-start = ((), (), s32[]{:S(2)}) async-start(), calls=%async_computation.14 | async-start | bytes 4423680 | tf_op jit(solution)/shard_map/reduce_scatter | solution.py:235
  399.0 150.8 %copy-start.1 = (bf16[1224,768]{1,0:T(8,128)(2,1)S(1)}, bf16[1224,768]{1,0:T(8,128)(2,1)}, u32[]{:S(2)}) copy-start(bf16[1224,768]{1,0:T(8,128)(2,1)} %param.20) | copy-start | bytes 5640196
  399.0 150.8 %copy-start.9 = (f32[1224]{0:T(1024)S(1)}, f32[1224]{0:T(1024)}, u32[]{:S(2)}) copy-start(f32[1224]{0:T(1024)} %copy-done.8) | copy-start | bytes 14692
  399.0 150.8 %copy-start.15 = (f32[1224]{0:T(1024)S(1)}, f32[1224]{0:T(1024)}, u32[]{:S(2)}) copy-start(f32[1224]{0:T(1024)} %copy-done.14) | copy-start | bytes 14692
  399.0 150.8 %copy-start.20 = (f32[768]{0:T(1024)S(1)}, f32[768]{0:T(1024)}, u32[]{:S(2)}) copy-start(f32[768]{0:T(1024)} %copy-done.19) | copy-start | bytes 9220
  399.1 150.8 %copy-start.33 = (f32[768]{0:T(1024)S(1)}, f32[768]{0:T(1024)}, u32[]{:S(2)}) copy-start(f32[768]{0:T(1024)} %copy-done.32) | copy-start | bytes 9220
  560.0 152.8 %reduce-scatter.21.cloned.1.call-start = ((), (), s32[]{:S(2)}) async-start(), calls=%async_computation.16 | async-start | bytes 5898240 | tf_op jit(solution)/shard_map/reduce_scatter | solution.py:241
  572.2 229.8 %reduce-scatter.23.cloned.1.call-start = ((), (), s32[]{:S(2)}) async-start(), calls=%async_computation.17 | async-start | bytes 5898240 | tf_op jit(solution)/shard_map/reduce_scatter | solution.py:244
  584.3 255.3 %reduce-scatter.27.cloned.1.call-start = ((), (), s32[]{:S(2)}) async-start(), calls=%async_computation.19 | async-start | bytes 442368
  589.1 38.2 %copy-start.13 = (f32[1224]{0:T(1024)S(1)}, f32[1224]{0:T(1024)}, u32[]{:S(2)}) copy-start(f32[1224]{0:T(1024)} %copy-done.12) | copy-start | bytes 14692
  589.1 290.3 %reduce-scatter.25.cloned.1.call-start = ((), (), s32[]{:S(2)}) async-start(), calls=%async_computation.18 | async-start | bytes 1327104
  627.2 294.3 %reduce-scatter.29.cloned.1.call-start = ((), (), s32[]{:S(2)}) async-start(), calls=%async_computation.20 | async-start | bytes 1769472
  631.0 84.4 %copy-start.24 = (f32[1224]{0:T(1024)S(1)}, f32[1224]{0:T(1024)}, u32[]{:S(2)}) copy-start(f32[1224]{0:T(1024)} %copy-done.23) | copy-start | bytes 14692
  715.3 246.4 %reduce-scatter.31.cloned.1.call-start = ((), (), s32[]{:S(2)}) async-start(), calls=%async_computation.21 | async-start | bytes 1327104
  (44 other events, 546.7 us)
Sparse Core Ops, SparseCore 0:
  9.9 27.3 all-gather.11
  39.2 24.6 all-gather.15
  66.0 70.0 all-gather.7
  138.1 29.0 all-gather.9
  168.6 88.5 all-gather.13
  258.6 87.8 all-gather.17
  387.8 27.5 reduce-scatter.18
  560.1 64.7 reduce-scatter.16
  627.2 85.5 reduce-scatter.20
  714.9 87.0 reduce-scatter.22
  805.1 34.3 reduce-scatter.26
  842.6 36.7 reduce-scatter.24
  883.0 38.4 reduce-scatter.28
  924.9 36.7 reduce-scatter.30
where the time goes:
time: 979 us; the launch traced here: 971 us
  waiting for transfers between devices  394 us (40%)
  matrix products  259 us (26%)
  local copies, waits for them, and re-layouts  113 us (12%)
  blocking collectives  113 us (12%)
  other arithmetic  69.5 us (7%)
  between operations  20.5 us (2%)
    unnamed x18, waiting for transfers between devices  142 us
    reduce_scatter x1, waiting for transfers between devices, per_device(): lax.psum_scatter(grad_w_up.astype(jnp.bfloat16), 'gx', scatter_dimension=...  79.2 us
    unnamed x5, blocking collectives  76.1 us
    all_gather x1, waiting for transfers between devices, per_device(): lax.all_gather(by_cols[3], 'gx', axis=0, tiled=True)  46.9 us
    dynamic_slice x48, local copies, waits for them, and re-layouts, per_device(): lax.map(attend, (query_blocks, key_blocks, value_blocks, pair_lengths))  43.8 us
    all_gather x1, waiting for transfers between devices, per_device(): lax.all_gather(by_cols[0], 'gx', axis=0, tiled=True)  43.1 us
    dot_general x1, matrix products, per_device(): jnp.dot(normed_two_low, mat_up, preferred_element_type=jnp.float32) + vec_up  42.4 us
    dot_general x12, matrix products, block_scores(): jnp.einsum('qhd,khd->hqk', query_heads, key_heads, preferred_element_type...  35.3 us
  transfers between devices with their start and end apart: 14, of which 11 were waited for; matrix products, arithmetic and copies ran while one was open for 41% of the time, Pallas kernels for 0%

commit v1 on v0

--- a/solution.py
+++ b/solution.py
@@ -7,6 +7,19 @@
 HEAD_DIM = 64
 EPSILON = 1e-06
 NEG_FILL = -1e30
+
+
+def gather_around(value, axis, dim):
+    ways = lax.axis_size(axis)
+    up = [(d, (d + 1) % ways) for d in range(ways)]
+    down = [(d, (d - 1) % ways) for d in range(ways)]
+    earlier, later = ([value], [value])
+    for _ in range(ways // 2):
+        earlier.append(lax.ppermute(earlier[-1], axis, up))
+    for _ in range((ways - 1) // 2):
+        later.append(lax.ppermute(later[-1], axis, down))
+    line = jnp.concatenate([*earlier[::-1], *later[1:]], axis=dim)
+    return jnp.roll(line, (lax.axis_index(axis) - ways // 2) * value.shape[dim], axis=dim)
 
 
 def layer_norm(values, gain_vec, shift_vec):
@@ -127,7 +140,7 @@
         lax.all_gather(shift_two, "gy", axis=0, tiled=True),
     )
     gathered = (
-        lax.all_gather(by_cols[0], "gx", axis=0, tiled=True),
+        gather_around(by_cols[0], "gx", 0),
         lax.all_gather(by_cols[1], "gx", axis=0, tiled=True),
         lax.all_gather(by_cols[2], "gx", axis=0, tiled=True),
         lax.all_gather(by_cols[3], "gx", axis=0, tiled=True),

time: 979 us -> 993 us (1.014)
  waiting for transfers between devices: 394 us -> 345 us
  blocking collectives: 113 us -> 144 us
  local copies, waits for them, and re-layouts: 113 us -> 131 us
    all_gather x1, waiting for transfers between devices: 43.1 us -> 0.02 us  [per_device(): lax.all_gather(regather_cols[0], 'gx', axis=0, tiled=True)]
    unnamed x5, blocking collectives: 76.1 us -> 106 us
    all_gather x1, waiting for transfers between devices: 25.5 us -> 10.3 us  [per_device(): lax.all_gather(by_cols[2], 'gx', axis=0, tiled=True)]
    concatenate x0 -> x1, local copies, waits for them, and re-layouts: none -> 13 us  [gather_around(): jnp.roll(line, (lax.axis_index(axis) - ways // 2) * value.shape[dim], axi...]
    ppermute x0 -> x3, waiting for transfers between devices: none -> 10.8 us  [the longest x2 10.8 us: gather_around(): earlier.append(lax.ppermute(earlier[-1], axis, up))]
    unnamed x156 -> x148, local copies, waits for them, and re-layouts: 25.6 us -> 23.2 us
  transfers between devices with their start and end apart: 14 -> 17, of which waited for: 11 -> 10; matrix products, arithmetic and copies ran while one was open for 41% -> 43% of each run, Pallas kernels for 0% -> 0%
where the time goes in v1:
time: 993 us; the launch traced here: 985 us
  waiting for transfers between devices  345 us (35%)
  matrix products  263 us (26%)
  blocking collectives  144 us (15%)
  local copies, waits for them, and re-layouts  131 us (13%)
  other arithmetic  75 us (8%)
  between operations  20.2 us (2%)
    unnamed x18, waiting for transfers between devices  142 us
    unnamed x5, blocking collectives  106 us
    reduce_scatter x1, waiting for transfers between devices, per_device(): lax.psum_scatter(grad_w_up.astype(jnp.bfloat16), 'gx', scatter_dimension=...  79.2 us
    all_gather x1, waiting for transfers between devices, per_device(): lax.all_gather(by_cols[3], 'gx', axis=0, tiled=True)  47.1 us
    dynamic_slice x48, local copies, waits for them, and re-layouts, per_device(): lax.map(attend, (query_blocks, key_blocks, value_blocks, pair_lengths))  43.8 us
    dot_general x1, matrix products, per_device(): jnp.dot(normed_two_low, mat_up, preferred_element_type=jnp.float32) + vec_up  42.2 us
    dot_general x12, matrix products, block_scores(): jnp.einsum('qhd,khd->hqk', query_heads, key_heads, preferred_element_type...  36.5 us
    reduce_scatter x1, waiting for transfers between devices, per_device(): lax.psum_scatter(grad_w_down.astype(jnp.bfloat16), 'gx', scatter_dimensio...  29.7 us
  transfers between devices with their start and end apart: 17, of which 10 were waited for; matrix products, arithmetic and copies ran while one was open for 43% of the time, Pallas kernels for 0%

profile of v1, /device:TPU:0, one launch (start us, length us, event | category | flops | bytes accessed | tf_op | source)
XLA Modules:
  0.0 984.8 jit_solution(18060099618871704560)
XLA Ops:
  9.0 11.0 %all_gather.94 = bf16[192,768]{0,1:T(8,128)(2,1)S(1)} all-gather(bf16[192,96]{0,1:T(8,128)(2,1)S(1)} %copy.76), channel_id=1, replica_groups=mesh['gx'=4,'gy'=8] {'gy'}, dimensions={1}, use_global_device_ids=true | all-gather | bytes 331776 | tf_op jit(solution)/shard_map/all_gather | solution.py:129
  22.0 13.6 %all_gather.89 = bf16[192,2304]{0,1:T(8,128)(2,1)S(1)} all-gather(bf16[192,288]{0,1:T(8,128)(2,1)S(1)} %copy.64), channel_id=1, replica_groups=mesh['gx'=4,'gy'=8] {'gy'}, dimensions={1}, use_global_device_ids=true | all-gather | bytes 995328 | tf_op jit(solution)/shard_map/all_gather | solution.py:128
  45.8 14.0 %all-reduce.36 = (bf16[768]{0:T(1024)(128)(2,1)S(1)}, bf16[192]{0:T(256)(128)(2,1)S(1)}, bf16[192]{0:T(256)(128)(2,1)S(1)}, bf16[192]{0:T(256)(128)(2,1)S(1)}, b...) all-reduce(bf16[768]{0:T(1024)(128)(2,1)S(1)} %dynamic-update-slice, ...), channel_id=1, replica_groups=mesh['gx'=4,'gy'=8] {'gy'}, use_global_device_ids=true, to_apply=%add.14 | all-reduce | flops 2112 | bytes 8448
  61.3 48.7 %all-reduce.38 = (bf16[768]{0:T(1024)(128)(2,1)S(1)}, bf16[768]{0:T(1024)(128)(2,1)S(1)}, bf16[768]{0:T(1024)(128)(2,1)S(1)}, bf16[768]{0:T(1024)(128)(2,1)S(1)}...) all-reduce(bf16[768]{0:T(1024)(128)(2,1)S(1)} %dynamic-update-slice, ...), channel_id=1, replica_groups=mesh['gx'=4,'gy'=8] {'gx'}, use_global_device_ids=true, to_apply=%add.7 | all-reduce | flops 5376 | bytes 21504
  110.8 13.1 %all-gather = bf16[4,1,768]{2,1,0:T(2,128)(2,1)S(1)} all-gather(bf16[1,1,768]{2,1,0:T(2,128)(2,1)S(1)} %reshape.302), channel_id=1, replica_groups=mesh['gx'=4,'gy'=8] {'gx'}, dimensions={0}, use_global_device_ids=true | all-gather | bytes 7680 | tf_op jit(solution)/shard_map/all_gather | solution.py:150
  131.4 10.8 %collective-permute-done.1 = bf16[192,2304]{1,0:T(8,128)(2,1)} collective-permute-done((bf16[192,2304]{1,0:T(8,128)(2,1)}, bf16[192,2304]{1,0:T(8,128)(2,1)}, u32[]{:S(2)}, u32[]{:S(2)}) %collective-permute-start.1) | collective-permute-done | bytes 884768 | tf_op jit(solution)/shard_map/ppermute | solution.py:18
  144.6 13.0 %concatenate.13 = bf16[1536,2304]{0,1:T(8,128)(2,1)} concatenate(bf16[192,2304]{0,1:T(8,128)(2,1)} %copy.67, bf16[192,2304]{0,1:T(8,128)(2,1)} %copy.68, bf16[192,2304]{0,1:T(8,128)(2,1)S(1)} %all_gather.89, bf16[192,2304]{0,1:T(8,128)(2,1)} %copy.69, bf16[192,2304]{0,1:T(8,128)(2,1)} %copy.67, bf16[192,2304]{0,1:T(8,128)(2,1)} %copy.68, bf16[192,2304]{0,1:T(8,128)(2,1)S(1)} %all_gather.89, ...), dimensions={0} | concatenate | bytes 14155776 | tf_op jit(solution)/shard_map/jit(_roll_dynamic)/concatenate | solution.py:22
  157.6 7.9 fusion.14
  181.7 65.9 %while.26 = (s32[]{:T(128)}, bf16[6,1224,128]{1,2,0:T(8,128)(2,1)}, f32[6,2,1224]{2,1,0:T(2,128)}, bf16[6,1224,128]{1,2,0:T(8,128)(2,1)}, s32[6]{0:T(128)S(1)}, ...) while((s32[]{:T(128)}, bf16[6,1224,128]{1,2,0:T(8,128)(2,1)}, ...), condition=%wide.region_5.6_spmd, body=%wide.region_2.5_spmd.sunk | while | flops 791035712 | bytes 39813052 | solution.py:176
  256.6 10.3 %all-gather.12.cloned.1.call-done = bf16[768,3072]{1,0:T(8,128)(2,1)} async-done(((bf16[192,3072]{1,0:T(8,128)(2,1)}), bf16[768,3072]{1,0:T(8,128)(2,1)}) %all-gather.12.cloned.1.call-update) | async-done | bytes 4718608 | tf_op jit(solution)/shard_map/all_gather | solution.py:145
  266.9 42.2 %multiply_convert_fusion.1 = (bf16[1224,3072]{1,0:T(8,128)(2,1)}, f32[1224,3072]{1,0:T(8,128)}, f32[1224,3072]{1,0:T(8,128)}) fusion(f32[3072]{0:T(1024)S(1)} %bitcast.195, bf16[768,3072]{1,0:T(8,128)(2,1)} %all-gather.12.cloned.1.call-done, f32[1224,768]{1,0:T(8,128)} %get-tuple-element.272, f32[768]{0:T(1024)S(1)} %convert_element_type.206, ...), kind=kOutput, calls=%fused_computation.34 | convolution fusion | flops 6028425216 | bytes 46108224 | tf_op jit(solution)/shard_map/dot_general | solution.py:183
  309.1 47.1 %all-gather.16.cloned.1.call-done = bf16[3072,768]{0,1:T(8,128)(2,1)} async-done(((bf16[768,768]{0,1:T(8,128)(2,1)}), bf16[3072,768]{0,1:T(8,128)(2,1)}) %all-gather.16.cloned.1.call-update) | async-done | bytes 4718608 | tf_op jit(solution)/shard_map/all_gather | solution.py:146
  356.2 19.9 %fusion.55 = (bf16[3072]{0:T(1024)(128)(2,1)}, bf16[1224,3072]{1,0:T(8,128)(2,1)}) fusion(f32[1224,3072]{1,0:T(8,128)} %get-tuple-element.252, f32[1224,3072]{1,0:T(8,128)} %get-tuple-element.273, bf16[3072,768]{0,1:T(8,128)(2,1)} %all-gather.16.cloned.1.call-done, bf16[1224,768]{1,0:T(8,128)(2,1)S(1)} %copy-done.4, f32[1224]{0:T(1024)S(1)} %copy-done.17), kind=kOutput, calls=%fused_computation.124 | convolution fusion | flops 5834775552 | bytes 44210976 | tf_op jit(solution)/shard_map/td,fd->tf/dot_general | solution.py:214
  376.1 12.4 %multiply_reduce_fusion.1 = (bf16[768]{0:T(1024)(128)(2,1)}, f32[1224]{0:T(1024)S(1)}, bf16[768]{0:T(1024)(128)(2,1)}, f32[1224,768]{1,0:T(8,128)S(1)}) fusion(f32[1224,768]{1,0:T(8,128)} %get-tuple-element.272, f32[1224]{0:T(1024)S(1)} %fusion.38, f32[1224]{0:T(1024)S(1)} %broadcast_multiply_fusion, f32[768]{0:T(1024)S(1)} %convert_element_type.205, ...), kind=kOutput, calls=%fused_computation.74 | convolution fusion | flops 5783073792 | bytes 19779936 | tf_op jit(solution)/shard_map/tf,df->td/dot_general | solution.py:218
  393.0 5.8 convolution_convert_fusion.4
  411.3 152.6 %while.27 = (s32[]{:T(128)}, bf16[6,1224,128]{1,2,0:T(8,128)(2,1)}, bf16[6,1224,128]{1,2,0:T(8,128)(2,1)}, bf16[6,1224,128]{1,2,0:T(8,128)(2,1)}, bf16[6,1224,12...) while((s32[]{:T(128)}, bf16[6,1224,128]{1,2,0:T(8,128)(2,1)}, ...), condition=%wide.region_12.13_spmd, body=%wide.region_10.12_spmd.sunk | while | flops 1945257856 | bytes 116307088 | solution.py:228
  564.0 10.1 %convolution_convert_fusion = bf16[768,2304]{1,0:T(8,128)(2,1)} fusion(bf16[1224,768]{1,0:T(8,128)(2,1)S(1)} %copy-done.1, f32[768]{0:T(1024)S(1)} %copy-done.27, f32[768]{0:T(1024)S(1)} %copy-done.16, f32[1224]{0:T(1024)S(1)} %copy-done.12, f32[1224]{0:T(1024)S(1)} %copy-done.6, bf16[1224,768]{0,1:T(8,128)(2,1)} %bitcast.183, ...), kind=kOutput, calls=%fused_computation.61 | convolution fusion | flops 4355997696 | bytes 11075136 | tf_op jit(solution)/shard_map/td,te->de/dot_general | solution.py:243
  574.3 12.1 %convolution_convert_fusion.2 = bf16[768,3072]{1,0:T(8,128)(2,1)} fusion(bf16[1224,3072]{1,0:T(8,128)(2,1)} %get-tuple-element.277, f32[1224,768]{1,0:T(8,128)} %get-tuple-element.272, f32[768]{0:T(1024)S(1)} %copy-done.29, f32[768]{0:T(1024)S(1)} %copy-done.24, f32[1224]{0:T(1024)S(1)} %copy-done.22, f32[1224]{0:T(1024)S(1)} %copy-done.14), kind=kOutput, calls=%fused_computation.63 | convolution fusion | flops 5782616064 | bytes 16014912 | tf_op jit(solution)/shard_map/td,tf->df/dot_general | solution.py:217
  587.1 11.3 %convolution_convert_fusion.1 = bf16[3072,768]{1,0:T(8,128)(2,1)} fusion(bf16[1224,3072]{1,0:T(8,128)(2,1)} %get-tuple-element.251, bf16[1224,768]{1,0:T(8,128)(2,1)} %param.22, f32[1224]{0:T(1024)S(1)} %copy-done.18), kind=kOutput, calls=%fused_computation.62 | convolution fusion | flops 5780736000 | bytes 14123808 | tf_op jit(solution)/shard_map/tf,td->fd/dot_general | solution.py:213
  603.3 10.1 %fusion.46 = (bf16[768]{0:T(1024)(128)(2,1)S(1)}, f32[1224]{0:T(1024)S(1)}, f32[1224,768]{1,0:T(8,128)}) fusion(f32[768]{0:T(1024)S(1)} %copy-done.16, f32[1224]{0:T(1024)S(1)} %copy-done.6, bf16[1224,768]{1,0:T(8,128)(2,1)S(1)} %copy-done.1, bf16[768,2304]{1,0:T(8,128)(2,1)} %all-gather.18.cloned.1.call-done, bf16[1224,768]{0,1:T(8,128)(2,1)} %bitcast.184, ...), kind=kOutput, calls=%fused_computation.116 | convolution fusion | flops 4354226176 | bytes 14833728 | tf_op jit(solution)/shard_map/te,de->td/dot_general | solution.py:244
  613.5 25.7 %reduce-scatter.17.cloned.1.call-done = bf16[192,2304]{1,0:T(8,128)(2,1)} async-done(((bf16[768,2304]{1,0:T(8,128)(2,1)}), bf16[192,2304]{1,0:T(8,128)(2,1)}) %reduce-scatter.17.cloned.1.call-update) | async-done | bytes 884752 | tf_op jit(solution)/shard_map/reduce_scatter | solution.py:248
  647.9 79.2 %reduce-scatter.21.cloned.1.call-done = bf16[192,3072]{1,0:T(8,128)(2,1)} async-done(((bf16[768,3072]{1,0:T(8,128)(2,1)}), bf16[192,3072]{1,0:T(8,128)(2,1)}) %reduce-scatter.21.cloned.1.call-update) | async-done | bytes 1179664 | tf_op jit(solution)/shard_map/reduce_scatter | solution.py:254
  729.7 7.2 fusion.28
  737.0 19.6 %all-reduce.37 = (bf16[768]{0:T(1024)(128)(2,1)S(1)}, bf16[768]{0:T(1024)(128)(2,1)S(1)}, bf16[768]{0:T(1024)(128)(2,1)S(1)}, bf16[3072]{0:T(1024)(128)(2,1)S(1)...) all-reduce(bf16[768]{0:T(1024)(128)(2,1)S(1)} %get-tuple-element.26, ...), channel_id=10, replica_groups=mesh['gx'=4,'gy'=8] {'gx'}, use_global_device_ids=true, to_apply=%region_24.25.clone | all-reduce | flops 9216 | bytes 36864
  757.3 13.2 %all-reduce.35 = (bf16[192]{0:T(256)(128)(2,1)S(1)}, bf16[192]{0:T(256)(128)(2,1)S(1)}, bf16[192]{0:T(256)(128)(2,1)S(1)}, bf16[192]{0:T(256)(128)(2,1)S(1)}, bf...) all-reduce(bf16[192]{0:T(256)(128)(2,1)S(1)} %dynamic-update-slice., ...), channel_id=1, replica_groups=mesh['gx'=4,'gy'=8] {'gy'}, use_global_device_ids=true, to_apply=%add.15 | all-reduce | flops 2496 | bytes 9984
  770.7 10.7 %all-reduce.16 = bf16[768]{0:T(1024)(128)(2,1)S(1)} all-reduce(bf16[768]{0:T(1024)(128)(2,1)S(1)} %dynamic-update-slice.16), channel_id=1, replica_groups=mesh['gx'=4,'gy'=8] {'gx'}, use_global_device_ids=true, to_apply=%add.16 | all-reduce | flops 768 | bytes 3072
  786.7 29.7 %reduce-scatter.23.cloned.1.call-done = bf16[768,768]{1,0:T(8,128)(2,1)} async-done(((bf16[3072,768]{1,0:T(8,128)(2,1)}), bf16[768,768]{1,0:T(8,128)(2,1)}) %reduce-scatter.23.cloned.1.call-update) | async-done | bytes 1179664 | tf_op jit(solution)/shard_map/reduce_scatter | solution.py:257
  818.8 11.3 %fusion.31 = bf16[1224,768]{1,0:T(8,128)(2,1)} fusion(f32[1224,768]{1,0:T(8,128)} %get-tuple-element.272, bf16[1224,3072]{1,0:T(8,128)(2,1)} %get-tuple-element.251, bf16[3072,768]{0,1:T(8,128)(2,1)} %all-gather.16.cloned.1.call-done, f32[768]{0:T(1024)S(1)} %convert_element_type.210), kind=kOutput, calls=%fused_computation.84 | convolution fusion | flops 5778376704 | bytes 17882112 | tf_op jit(solution)/shard_map/dot_general | solution.py:187
  830.1 23.7 %reduce-scatter.27.cloned.1.call-done = bf16[96,192]{1,0:T(8,128)(2,1)} async-done(((bf16[768,192]{1,0:T(8,128)(2,1)}), bf16[96,192]{1,0:T(8,128)(2,1)}) %reduce-scatter.27.cloned.1.call-update) | async-done | bytes 36880
  855.4 38.3 %reduce-scatter.25.cloned.1.call-done = bf16[288,192]{1,0:T(8,128)(2,1)} async-done(((bf16[2304,192]{1,0:T(8,128)(2,1)}), bf16[288,192]{1,0:T(8,128)(2,1)}) %reduce-scatter.25.cloned.1.call-update) | async-done | bytes 110608
  895.5 40.3 %reduce-scatter.29.cloned.1.call-done = bf16[384,192]{1,0:T(8,128)(2,1)} async-done(((bf16[3072,192]{1,0:T(8,128)(2,1)}), bf16[384,192]{1,0:T(8,128)(2,1)}) %reduce-scatter.29.cloned.1.call-update) | async-done | bytes 147472
  937.6 38.4 %reduce-scatter.31.cloned.1.call-done = bf16[96,768]{1,0:T(8,128)(2,1)} async-done(((bf16[768,768]{1,0:T(8,128)(2,1)}), bf16[96,768]{1,0:T(8,128)(2,1)}) %reduce-scatter.31.cloned.1.call-update) | async-done | bytes 147472
  (417 shorter events, 313.0 us)
Async XLA Ops:
  7.3 117.8 %copy-start = (bf16[1224,768]{1,0:T(8,128)(2,1)S(1)}, bf16[1224,768]{1,0:T(8,128)(2,1)}, u32[]{:S(2)}) copy-start(bf16[1224,768]{1,0:T(8,128)(2,1)} %param.20) | copy-start | bytes 5640196
  7.3 172.8 %all-gather.10.cloned.1.call-start = ((), (), s32[]{:S(2)}) async-start(), calls=%async_computation.9 | async-start | bytes 1327104 | tf_op jit(solution)/shard_map/all_gather | solution.py:130
  8.0 239.6 %all-gather.8.cloned.1.call-start = ((), (), s32[]{:S(2)}) async-start(), calls=%async_computation.8 | async-start | bytes 1474560 | tf_op jit(solution)/shard_map/all_gather | solution.py:144
  20.9 235.4 %all-gather.14.cloned.1.call-start = ((), (), s32[]{:S(2)}) async-start(), calls=%async_computation.11 | async-start | bytes 1327104 | tf_op jit(solution)/shard_map/all_gather | solution.py:131
  36.9 87.6 %collective-permute-start = (bf16[192,2304]{1,0:T(8,128)(2,1)}, bf16[192,2304]{1,0:T(8,128)(2,1)}, u32[]{:S(2)}, u32[]{:S(2)}) collective-permute-start(bf16[192,2304]{1,0:T(8,128)(2,1)} %copy.65), channel_id=1, source_target_pairs={{0,8},{8,16},{16,24},{24,0},{1,9},{9,17},{17,25},{25,1},{2,10},{10... | collective-permute-start | bytes 2654216 | tf_op jit(solution)/shard_map/ppermute | solution.py:18
  38.7 90.4 %collective-permute-start.2 = (bf16[192,2304]{1,0:T(8,128)(2,1)}, bf16[192,2304]{1,0:T(8,128)(2,1)}, u32[]{:S(2)}, u32[]{:S(2)}) collective-permute-start(bf16[192,2304]{1,0:T(8,128)(2,1)} %copy.65), channel_id=1, source_target_pairs={{0,24},{8,0},{16,8},{24,16},{1,25},{9,1},{17,9},{25,17},{2,26},{10... | collective-permute-start | bytes 2654216 | tf_op jit(solution)/shard_map/ppermute | solution.py:20
  41.1 225.8 %all-gather.12.cloned.1.call-start = ((), (), s32[]{:S(2)}) async-start(), calls=%async_computation.10 | async-start | bytes 5898240 | tf_op jit(solution)/shard_map/all_gather | solution.py:145
  110.0 47.5 %copy-start.15 = (f32[768]{0:T(1024)}, f32[768]{0:T(1024)S(1)}, u32[]{:S(2)}) copy-start(f32[768]{0:T(1024)S(1)} %convert_element_type.194) | copy-start | bytes 9220
  110.0 47.5 %copy-start.26 = (f32[768]{0:T(1024)}, f32[768]{0:T(1024)S(1)}, u32[]{:S(2)}) copy-start(f32[768]{0:T(1024)S(1)} %convert_element_type.195) | copy-start | bytes 9220
  110.7 277.8 %copy-start.23 = (f32[768]{0:T(1024)}, f32[768]{0:T(1024)S(1)}, u32[]{:S(2)}) copy-start(f32[768]{0:T(1024)S(1)} %convert_element_type.205) | copy-start | bytes 9220
  110.8 156.2 %copy-start.28 = (f32[768]{0:T(1024)}, f32[768]{0:T(1024)S(1)}, u32[]{:S(2)}) copy-start(f32[768]{0:T(1024)S(1)} %convert_element_type.206) | copy-start | bytes 9220
  124.5 17.7 %collective-permute-start.1 = (bf16[192,2304]{1,0:T(8,128)(2,1)}, bf16[192,2304]{1,0:T(8,128)(2,1)}, u32[]{:S(2)}, u32[]{:S(2)}) collective-permute-start(bf16[192,2304]{1,0:T(8,128)(2,1)} %collective-permute-done), channel_id=1, source_target_pairs={{0,8},{8,16},{16,24},{24,0},{1,9},{9,17},{17,25},{25,1},{2,10},{10... | collective-permute-start | bytes 2654216 | tf_op jit(solution)/shard_map/ppermute | solution.py:18
  180.1 176.1 %all-gather.16.cloned.1.call-start = ((), (), s32[]{:S(2)}) async-start(), calls=%async_computation.12 | async-start | bytes 5898240 | tf_op jit(solution)/shard_map/all_gather | solution.py:146
  253.1 135.4 %copy-start.13 = (f32[1224]{0:T(1024)}, f32[1224]{0:T(1024)S(1)}, u32[]{:S(2)}) copy-start(f32[1224]{0:T(1024)S(1)} %broadcast_multiply_fusion) | copy-start | bytes 14692
  256.3 132.2 %copy-start.21 = (f32[1224]{0:T(1024)}, f32[1224]{0:T(1024)S(1)}, u32[]{:S(2)}) copy-start(f32[1224]{0:T(1024)S(1)} %fusion.38) | copy-start | bytes 14692
  256.3 345.0 %reduce-scatter.19.cloned.1.call-start = ((), (), s32[]{:S(2)}) async-start(), calls=%async_computation.15 | async-start | bytes 1474560 | tf_op jit(solution)/shard_map/reduce_scatter | solution.py:251
  266.9 89.3 %copy-start.4 = (bf16[1224,768]{1,0:T(8,128)(2,1)S(1)}, bf16[1224,768]{1,0:T(8,128)(2,1)}, u32[]{:S(2)}) copy-start(bf16[1224,768]{1,0:T(8,128)(2,1)} %param.22) | copy-start | bytes 5640196
  266.9 89.3 %copy-start.17 = (f32[1224]{0:T(1024)S(1)}, f32[1224]{0:T(1024)}, u32[]{:S(2)}) copy-start(f32[1224]{0:T(1024)} %fusion.36) | copy-start | bytes 14692
  398.9 204.4 %all-gather.18.cloned.1.call-start = ((), (), s32[]{:S(2)}) async-start(), calls=%async_computation.13 | async-start | bytes 4423680 | tf_op jit(solution)/shard_map/all_gather | solution.py:196
  399.7 239.5 %reduce-scatter.17.cloned.1.call-start = ((), (), s32[]{:S(2)}) async-start(), calls=%async_computation.14 | async-start | bytes 4423680 | tf_op jit(solution)/shard_map/reduce_scatter | solution.py:248
  411.3 152.6 %copy-start.1 = (bf16[1224,768]{1,0:T(8,128)(2,1)S(1)}, bf16[1224,768]{1,0:T(8,128)(2,1)}, u32[]{:S(2)}) copy-start(bf16[1224,768]{1,0:T(8,128)(2,1)} %param.20) | copy-start | bytes 5640196
  411.3 152.6 %copy-start.6 = (f32[1224]{0:T(1024)S(1)}, f32[1224]{0:T(1024)}, u32[]{:S(2)}) copy-start(f32[1224]{0:T(1024)} %copy-done.5) | copy-start | bytes 14692
  411.3 152.7 %copy-start.12 = (f32[1224]{0:T(1024)S(1)}, f32[1224]{0:T(1024)}, u32[]{:S(2)}) copy-start(f32[1224]{0:T(1024)} %copy-done.11) | copy-start | bytes 14692
  411.3 152.7 %copy-start.16 = (f32[768]{0:T(1024)S(1)}, f32[768]{0:T(1024)}, u32[]{:S(2)}) copy-start(f32[768]{0:T(1024)} %copy-done.15) | copy-start | bytes 9220
  411.3 152.7 %copy-start.27 = (f32[768]{0:T(1024)S(1)}, f32[768]{0:T(1024)}, u32[]{:S(2)}) copy-start(f32[768]{0:T(1024)} %copy-done.26) | copy-start | bytes 9220
  574.2 152.9 %reduce-scatter.21.cloned.1.call-start = ((), (), s32[]{:S(2)}) async-start(), calls=%async_computation.16 | async-start | bytes 5898240 | tf_op jit(solution)/shard_map/reduce_scatter | solution.py:254
  586.4 229.9 %reduce-scatter.23.cloned.1.call-start = ((), (), s32[]{:S(2)}) async-start(), calls=%async_computation.17 | async-start | bytes 5898240 | tf_op jit(solution)/shard_map/reduce_scatter | solution.py:257
  598.4 255.4 %reduce-scatter.27.cloned.1.call-start = ((), (), s32[]{:S(2)}) async-start(), calls=%async_computation.19 | async-start | bytes 442368
  603.3 290.4 %reduce-scatter.25.cloned.1.call-start = ((), (), s32[]{:S(2)}) async-start(), calls=%async_computation.18 | async-start | bytes 1327104
  641.5 294.3 %reduce-scatter.29.cloned.1.call-start = ((), (), s32[]{:S(2)}) async-start(), calls=%async_computation.20 | async-start | bytes 1769472
  645.4 84.3 %copy-start.20 = (f32[1224]{0:T(1024)S(1)}, f32[1224]{0:T(1024)}, u32[]{:S(2)}) copy-start(f32[1224]{0:T(1024)} %copy-done.19) | copy-start | bytes 14692
  729.6 246.4 %reduce-scatter.31.cloned.1.call-start = ((), (), s32[]{:S(2)}) async-start(), calls=%async_computation.21 | async-start | bytes 1327104
  (43 other events, 638.8 us)
Sparse Core Ops, SparseCore 0:
  10.0 27.7 all-gather.9
  39.9 50.4 all-gather.7
  92.3 31.7 all-gather.13
  180.2 86.6 all-gather.11
  268.3 87.8 all-gather.15
  399.0 27.5 reduce-scatter.18
  428.2 68.7 all-gather.17
  574.3 64.8 reduce-scatter.16
  641.5 85.5 reduce-scatter.20
  729.2 87.0 reduce-scatter.22
  819.4 34.3 reduce-scatter.26
  856.9 36.7 reduce-scatter.24
  897.3 38.4 reduce-scatter.28
  939.2 36.7 reduce-scatter.30
